TPU v7x, 32 devices: a whole 2x2x4 slice. The times are simulated.
32 devices in a mesh: dp: 8 (over z, x), seq: 4 (over y, core).
Axes of the slice: x: 2, y: 2, z: 4, core: 2. Of those that a mesh axis runs over, the one named last changes fastest.
Arguments:
- field: bfloat16 [8, 2048, 1024], P('dp', 'seq'), may hold values from -6 to 6
- eq_embed: bfloat16 [8, 512, 1024], P('dp', 'seq'), may hold values from -6 to 6
- eq_len: int32 [8], replicated, may hold values from 1 to 512, 2048 in all
- owner: int32 [8], replicated, may hold values from 0 to 7, as said below
- norm_gain: float32 [1024], replicated, may hold values from 0.1 to 1.9
- w_qkv: bfloat16 [1024, 3072], replicated, may hold values from -0.176776695 to 0.176776695
- w_out: bfloat16 [1024, 1024], replicated, may hold values from -0.1875 to 0.1875
- cross_gain: float32 [1024], replicated, may hold values from 0.1 to 1.9
- w_cq: bfloat16 [1024, 1024], replicated, may hold values from -0.125 to 0.125
- w_ckv: bfloat16 [1024, 2048], replicated, may hold values from -0.125 to 0.125
- w_cout: bfloat16 [1024, 1024], replicated, may hold values from -0.1875 to 0.1875
Outputs:
- joined: bfloat16 [8, 2048, 1024], P('dp', 'seq')
Inputs may be any that keep to these rules, and one draw needn't show every extreme that they name: `owner`: every slot number appears exactly once. `eq_len`: some slot has all 512 tokens real.
All inputs are finite; a program needn't handle non-finite values.
Results may differ from a plain program's by a relative error of at most 0.0055.
Values may be sent and summed in bfloat16 or wider, within the bound.
A program may use at most 128 MiB of HBM per device.

v0:
```python
import jax
import jax.numpy as jnp
from jax import lax
from jax.sharding import PartitionSpec as P

D = 1024
HEADS = 16
HEAD_DIM = 64


def normalize(values, gain):
    return values * lax.rsqrt(jnp.mean(values * values, axis=-1, keepdims=True) + 1e-06) * gain


def attend(query, keys, values, valid):
    rows = query.shape[0]
    heads = query.shape[1]
    depth = query.shape[2]
    block = min(512, rows)
    scale = depth ** (-0.5)

    def one_block(query_block):
        scores = (
            jnp.einsum("qhd,khd->hqk", query_block, keys, preferred_element_type=jnp.float32)
            * scale
        )
        expo = jnp.where(valid[None, None, :], jnp.exp(scores), 0.0)
        weights = (expo / jnp.sum(expo, axis=-1, keepdims=True)).astype(jnp.bfloat16)
        return jnp.einsum(
            "hqk,khd->qhd", weights, values, preferred_element_type=jnp.float32
        ).astype(jnp.bfloat16)

    blocks = lax.map(one_block, query.reshape(rows // block, block, heads, depth))
    return blocks.reshape(rows, heads * depth)


def pick_slot(wanted, carry, piece):
    inside = (wanted >= 0) & (wanted < piece.shape[0])
    picked = lax.dynamic_index_in_dim(
        piece, jnp.clip(wanted, 0, piece.shape[0] - 1), 0, keepdims=False
    )
    return jnp.where(inside, picked, carry)


def per_device(
    field, eq_embed, eq_len, owner, norm_gain, w_qkv, w_out, cross_gain, w_cq, w_ckv, w_cout
):
    tokens = field[0].astype(jnp.float32)
    tok_rows = tokens.shape[0]
    groups = lax.axis_size("seq")
    head_count = HEADS // groups
    normed = normalize(tokens, norm_gain).astype(jnp.bfloat16)
    projected = jnp.dot(normed, w_qkv, preferred_element_type=jnp.float32).astype(jnp.bfloat16)
    stacked = projected.reshape(tok_rows, 3, D)
    local_heads = lax.all_to_all(stacked, "seq", split_axis=2, concat_axis=0, tiled=True)
    seq_rows = local_heads.shape[0]
    split = local_heads.reshape(seq_rows, 3, head_count, HEAD_DIM)
    every = jnp.ones((seq_rows,), dtype=bool)
    attended = attend(split[:, 0], split[:, 1], split[:, 2], every)
    merged = lax.all_to_all(attended, "seq", split_axis=0, concat_axis=1, tiled=True)
    mixed = tokens + jnp.dot(merged, w_out, preferred_element_type=jnp.float32)
    cross_in = normalize(mixed, cross_gain).astype(jnp.bfloat16)
    cross_q = jnp.dot(cross_in, w_cq, preferred_element_type=jnp.float32).astype(jnp.bfloat16)
    slot = lax.dynamic_index_in_dim(owner, lax.axis_index("dp"), 0, keepdims=False)
    length = lax.dynamic_index_in_dim(eq_len, slot, 0, keepdims=False)
    eq_rows = eq_embed.shape[1]
    empty = jnp.zeros(eq_embed.shape[1:], jnp.bfloat16)
    owned_rows = pick_slot(slot, empty, lax.all_gather(eq_embed, "dp", axis=0, tiled=True))
    owned_kv = jnp.dot(owned_rows, w_ckv, preferred_element_type=jnp.float32).astype(jnp.bfloat16)
    whole_kv = lax.all_gather(owned_kv, "seq", axis=0, tiled=True)
    whole_kv = whole_kv.reshape(eq_rows * groups, 2, HEADS, HEAD_DIM)
    valid = jnp.arange(eq_rows * groups, dtype=jnp.int32) < length
    cross_att = attend(
        cross_q.reshape(tok_rows, HEADS, HEAD_DIM), whole_kv[:, 0], whole_kv[:, 1], valid
    )
    joined = mixed + jnp.dot(cross_att, w_cout, preferred_element_type=jnp.float32)
    return joined.astype(jnp.bfloat16)[None]


def solution(mesh):
    in_specs = (
        P("dp", "seq", None),
        P("dp", "seq", None),
        P(),
        P(),
        P(),
        P(),
        P(),
        P(),
        P(),
        P(),
        P(),
    )
    out_specs = P("dp", "seq", None)
    return jax.shard_map(
        per_device, mesh=mesh, in_specs=in_specs, out_specs=out_specs, check_vma=False
    )
```

profile of v0, /device:TPU:0, one launch (start us, length us, event | category | flops | bytes accessed | tf_op | source)
XLA Modules:
  0.0 189.4 jit_solution(14081409868850262506)
XLA Ops:
  6.5 0.0 copy-start
  6.5 0.0 all-gather.3.cloned.1.call-start
  6.5 0.7 all-gather.3.cloned.1.call-update
  7.3 1.5 fusion.12
  8.8 8.3 %convolution_convert_fusion = bf16[512,3072]{1,0:T(8,128)(2,1)} fusion(bf16[1024,3072]{1,0:T(8,128)(2,1)} %param.18, bf16[1,512,1024]{2,1,0:T(8,128)(2,1)} %param.13, f32[1024]{0:T(1024)} %param.17, f32[512]{0:T(512)S(1)} %add_rsqrt_fusion.1), kind=kOutput, calls=%fused_computation.16 | convolution fusion | flops 3224895488 | bytes 10491904 | tf_op jit(solution)/shard_map/dot_general | solution.py:53
  17.1 4.7 %copy.28 = bf16[512,3072]{0,1:T(8,128)(2,1)} copy(bf16[512,3072]{1,0:T(8,128)(2,1)} %convolution_convert_fusion) | data formatting | bytes 6291456 | tf_op jit(solution)/shard_map/convert_element_type | solution.py:53
  21.7 6.5 %copy.29 = bf16[512,3,1024]{0,1,2:T(4,128)(2,1)} copy(bf16[512,3,1024]{0,2,1:T(8,128)(2,1)} %bitcast.75) | data formatting | bytes 6291456 | tf_op jit(solution)/shard_map/reshape | solution.py:54
  28.3 5.0 %all-to-all-start = ((bf16[512,3,1024]{0,1,2:T(4,128)(2,1)}), bf16[512,3,1024]{0,1,2:T(4,128)(2,1)}, u32[]{:S(2)}, u32[]{:S(2)}) async-start(bf16[512,3,1024]{0,1,2:T(4,128)(2,1)} %copy.29), calls=%async_computation | async-start | bytes 8388608 | tf_op jit(solution)/shard_map/all_to_all | solution.py:55
  33.3 0.2 all-gather.5.cloned.1.call-start
  33.5 0.0 copy-done.8
  33.5 0.6 dynamic_slice.18
  35.8 46.4 %all-to-all-done = bf16[512,3,1024]{0,1,2:T(4,128)(2,1)} async-done(((bf16[512,3,1024]{0,1,2:T(4,128)(2,1)}), bf16[512,3,1024]{0,1,2:T(4,128)(2,1)}, u32[]{:S(2)}, u32[]{:S(2)}) %all-to-all-start) | async-done | bytes 3145760 | tf_op jit(solution)/shard_map/all_to_all | solution.py:55
  82.2 3.0 %copy.30 = bf16[512,3,1024]{0,2,1:T(8,128)(2,1)S(1)} copy(bf16[512,3,1024]{0,1,2:T(4,128)(2,1)} %all-to-all-done) | data formatting | bytes 6291456 | tf_op jit(solution)/shard_map/all_to_all | solution.py:55
  85.1 4.1 %copy.31 = bf16[4,512,3,256]{1,0,3,2:T(4,128)(2,1)} copy(bf16[4,512,3,256]{1,3,0,2:T(8,128)(2,1)S(1)} %bitcast.76) | data formatting | bytes 6291456 | tf_op jit(solution)/shard_map/all_to_all | solution.py:55
  89.2 6.1 %reshape.50 = bf16[2048,3,4,64]{0,3,2,1:T(8,128)(2,1)} reshape(bf16[4,512,3,256]{1,0,3,2:T(4,128)(2,1)} %copy.31) | data formatting | bytes 6291456 | tf_op jit(solution)/shard_map/reshape | solution.py:57
  95.3 3.6 %slice_bitcast_fusion.4 = (bf16[2048,4,64]{0,2,1:T(8,128)(2,1)}, bf16[2048,4,64]{0,2,1:T(8,128)(2,1)S(1)}, bf16[2048,1,4,64]{0,3,2,1:T(8,128)(2,1)}) fusion(bf16[2048,3,4,64]{0,3,2,1:T(8,128)(2,1)} %reshape.50), kind=kLoop, calls=%fused_computation.33 | loop fusion | bytes 6291456 | tf_op jit(solution)/shard_map/squeeze | solution.py:59
  98.9 2.6 %reshape_squeeze.3 = bf16[4,512,4,64]{1,0,3,2:T(4,128)(2,1)} reshape(bf16[2048,1,4,64]{0,3,2,1:T(8,128)(2,1)} %get-tuple-element.80) | data formatting | bytes 2097152 | tf_op jit(solution)/shard_map/reshape;squeeze | solution.py:33
  101.5 2.4 %copy.32 = bf16[4,512,4,64]{1,3,2,0:T(8,128)(2,1)} copy(bf16[4,512,4,64]{1,0,3,2:T(4,128)(2,1)} %reshape_squeeze.3) | data formatting | bytes 2097152 | tf_op jit(solution)/shard_map/while | solution.py:33
  103.9 3.8 %convolution_convert_fusion.1 = bf16[128,2048]{1,0:T(8,128)(2,1)} fusion(bf16[1024,2048]{1,0:T(8,128)(2,1)} %param.22, bf16[8,128,1024]{2,1,0:T(8,128)(2,1)} %all-gather.3.cloned.1.call-done, s32[]{:T(128)S(6)} %min.4, pred[]{:T(512)S(6)} %and.4), kind=kOutput, calls=%fused_computation.20 | convolution fusion | flops 537264128 | bytes 4980741 | tf_op jit(solution)/shard_map/dot_general | solution.py:69
  107.7 0.0 all-gather.5.cloned.1.call-update
  107.8 0.0 copy-start.9
  107.8 33.5 %while.2 = (s32[]{:T(128)}, bf16[4,512,4,64]{1,3,2,0:T(8,128)(2,1)}, bf16[4,512,4,64]{1,3,2,0:T(8,128)(2,1)}, bf16[2048,4,64]{0,2,1:T(8,128)(2,1)S(1)}, bf16[2048,4,64]{0,2,1:T(8,128)(2,1)}, /*index=5*/s32[]{:T(128)}) while((s32[]{:T(128)}, bf16[4,512,4,64]{1,3,2,0:T(8,128)(2,1)}, bf16[4,512,4,64]{1,3,2,0:T(8,128)(2,1)}, ...), condition=%wide.region_3.4_spmd, body=%wide.region_1.3_spmd.sunk | while | flops 1094842368 | bytes 40386672 | solution.py:33
  107.8 0.0 copy-start.4
  107.8 4.0 %fusion.49 = (f32[4,512]{1,0:T(4,128)S(1)}, f32[4,512,2048]{2,1,0:T(8,128)S(1)}) fusion(bf16[2048,4,64]{0,2,1:T(8,128)(2,1)S(1)} %get-tuple-element.135, bf16[4,512,4,64]{1,3,2,0:T(8,128)(2,1)} %get-tuple-element.134, s32[]{:T(128)S(6)} %copy.40), kind=kOutput, calls=%fused_computation.2.clone.1 | convolution fusion | flops 545257472 | bytes 18096132 | tf_op jit(solution)/shard_map/while/body/eval_jaxpr/qhd,khd->hqk/dot_general | solution.py:24
  111.8 0.0 copy-done.4
  111.9 4.3 %fusion.50 = bf16[4,512,4,64]{1,3,2,0:T(8,128)(2,1)} fusion(bf16[4,512,4,64]{1,3,2,0:T(8,128)(2,1)} %get-tuple-element.127, s32[]{:T(128)S(6)} %copy.40, bf16[2048,4,64]{0,2,1:T(8,128)(2,1)S(1)} %copy-done.4, f32[4,512,2048]{2,1,0:T(8,128)S(1)} %get-tuple-element.118, f32[4,512]{1,0:T(4,128)S(1)} %get-tuple-element.119), kind=kOutput, calls=%fused_computation.6.clone.1 | convolution fusion | flops 549584896 | bytes 18096132 | tf_op jit(solution)/shard_map/while/body/eval_jaxpr/hqk,khd->qhd/dot_general | solution.py:29
  116.2 4.1 %fusion.49 = (f32[4,512]{1,0:T(4,128)S(1)}, f32[4,512,2048]{2,1,0:T(8,128)S(1)}) fusion(bf16[2048,4,64]{0,2,1:T(8,128)(2,1)S(1)} %get-tuple-element.135, bf16[4,512,4,64]{1,3,2,0:T(8,128)(2,1)} %get-tuple-element.134, s32[]{:T(128)S(6)} %copy.40), kind=kOutput, calls=%fused_computation.2.clone.1 | convolution fusion | flops 545257472 | bytes 18096132 | tf_op jit(solution)/shard_map/while/body/eval_jaxpr/qhd,khd->hqk/dot_general | solution.py:24
  120.3 0.0 copy-done.4
  120.3 4.3 %fusion.50 = bf16[4,512,4,64]{1,3,2,0:T(8,128)(2,1)} fusion(bf16[4,512,4,64]{1,3,2,0:T(8,128)(2,1)} %get-tuple-element.127, s32[]{:T(128)S(6)} %copy.40, bf16[2048,4,64]{0,2,1:T(8,128)(2,1)S(1)} %copy-done.4, f32[4,512,2048]{2,1,0:T(8,128)S(1)} %get-tuple-element.118, f32[4,512]{1,0:T(4,128)S(1)} %get-tuple-element.119), kind=kOutput, calls=%fused_computation.6.clone.1 | convolution fusion | flops 549584896 | bytes 18096132 | tf_op jit(solution)/shard_map/while/body/eval_jaxpr/hqk,khd->qhd/dot_general | solution.py:29
  124.6 4.0 %fusion.49 = (f32[4,512]{1,0:T(4,128)S(1)}, f32[4,512,2048]{2,1,0:T(8,128)S(1)}) fusion(bf16[2048,4,64]{0,2,1:T(8,128)(2,1)S(1)} %get-tuple-element.135, bf16[4,512,4,64]{1,3,2,0:T(8,128)(2,1)} %get-tuple-element.134, s32[]{:T(128)S(6)} %copy.40), kind=kOutput, calls=%fused_computation.2.clone.1 | convolution fusion | flops 545257472 | bytes 18096132 | tf_op jit(solution)/shard_map/while/body/eval_jaxpr/qhd,khd->hqk/dot_general | solution.py:24
  128.6 4.3 %fusion.50 = bf16[4,512,4,64]{1,3,2,0:T(8,128)(2,1)} fusion(bf16[4,512,4,64]{1,3,2,0:T(8,128)(2,1)} %get-tuple-element.127, s32[]{:T(128)S(6)} %copy.40, bf16[2048,4,64]{0,2,1:T(8,128)(2,1)S(1)} %copy-done.4, f32[4,512,2048]{2,1,0:T(8,128)S(1)} %get-tuple-element.118, f32[4,512]{1,0:T(4,128)S(1)} %get-tuple-element.119), kind=kOutput, calls=%fused_computation.6.clone.1 | convolution fusion | flops 549584896 | bytes 18096132 | tf_op jit(solution)/shard_map/while/body/eval_jaxpr/hqk,khd->qhd/dot_general | solution.py:29
  132.9 4.0 %fusion.49 = (f32[4,512]{1,0:T(4,128)S(1)}, f32[4,512,2048]{2,1,0:T(8,128)S(1)}) fusion(bf16[2048,4,64]{0,2,1:T(8,128)(2,1)S(1)} %get-tuple-element.135, bf16[4,512,4,64]{1,3,2,0:T(8,128)(2,1)} %get-tuple-element.134, s32[]{:T(128)S(6)} %copy.40), kind=kOutput, calls=%fused_computation.2.clone.1 | convolution fusion | flops 545257472 | bytes 18096132 | tf_op jit(solution)/shard_map/while/body/eval_jaxpr/qhd,khd->hqk/dot_general | solution.py:24
  137.0 0.0 copy-done.4
  137.0 4.3 %fusion.50 = bf16[4,512,4,64]{1,3,2,0:T(8,128)(2,1)} fusion(bf16[4,512,4,64]{1,3,2,0:T(8,128)(2,1)} %get-tuple-element.127, s32[]{:T(128)S(6)} %copy.40, bf16[2048,4,64]{0,2,1:T(8,128)(2,1)S(1)} %copy-done.4, f32[4,512,2048]{2,1,0:T(8,128)S(1)} %get-tuple-element.118, f32[4,512]{1,0:T(4,128)S(1)} %get-tuple-element.119), kind=kOutput, calls=%fused_computation.6.clone.1 | convolution fusion | flops 549584896 | bytes 18096132 | tf_op jit(solution)/shard_map/while/body/eval_jaxpr/hqk,khd->qhd/dot_general | solution.py:29
  141.3 3.7 %all-to-all-start.1 = ((bf16[4,512,256]{1,2,0:T(8,128)(2,1)}), bf16[4,512,256]{1,2,0:T(8,128)(2,1)S(1)}, u32[]{:S(2)}, u32[]{:S(2)}) async-start(bf16[4,512,256]{1,2,0:T(8,128)(2,1)} %bitcast.80), calls=%async_computation.1 | async-start | bytes 2097152 | tf_op jit(solution)/shard_map/all_to_all | solution.py:60
  146.7 0.6 dynamic_slice.20
  147.3 0.6 iota_compare_fusion
  148.0 11.3 %all-to-all-done.1 = bf16[4,512,256]{1,2,0:T(8,128)(2,1)S(1)} async-done(((bf16[4,512,256]{1,2,0:T(8,128)(2,1)}), bf16[4,512,256]{1,2,0:T(8,128)(2,1)S(1)}, u32[]{:S(2)}, u32[]{:S(2)}) %all-to-all-start.1) | async-done | bytes 1048608 | tf_op jit(solution)/shard_map/all_to_all | solution.py:60
  159.2 2.7 %multiply_reduce_fusion = (f32[512]{0:T(512)S(1)}, f32[512,1024]{1,0:T(8,128)S(1)}) fusion(bf16[512,1024]{0,1:T(8,128)(2,1)S(1)} %bitcast.77, bf16[1024,1024]{1,0:T(8,128)(2,1)S(1)} %copy-done, bf16[1,512,1024]{2,1,0:T(8,128)(2,1)} %param.13), kind=kOutput, calls=%fused_computation.26 | convolution fusion | flops 1075838464 | bytes 6293504 | tf_op jit(solution)/shard_map/dot_general | solution.py:61
  162.0 1.3 copy-done.1
  163.3 2.3 %convolution_convert_fusion.2 = bf16[512,1024]{1,0:T(8,128)(2,1)} fusion(bf16[1024,1024]{1,0:T(8,128)(2,1)S(1)} %copy-done.5, f32[512,1024]{1,0:T(8,128)S(1)} %get-tuple-element.82, f32[1024]{0:T(1024)S(1)} %copy-done.7, f32[512]{0:T(512)S(1)} %add_rsqrt_fusion), kind=kOutput, calls=%fused_computation.28 | convolution fusion | flops 1075838976 | bytes 5249024 | tf_op jit(solution)/shard_map/dot_general | solution.py:63
  165.6 1.5 copy.34
  167.1 0.0 all-gather.5.cloned.1.call-done
  167.1 3.9 %copy.33 = bf16[512,2048]{0,1:T(8,128)(2,1)} copy(bf16[512,2048]{1,0:T(8,128)(2,1)} %all-gather.5.cloned.1.call-done) | data formatting | bytes 4194304 | tf_op jit(solution)/shard_map/all_gather | solution.py:70
  171.0 5.5 %fusion.10 = (f32[16,512]{1,0:T(8,128)S(1)}, f32[16,512,512]{1,2,0:T(8,128)S(1)}) fusion(pred[512]{0:T(512)(128)(4,1)S(1)} %iota_compare_fusion, bf16[512,16,64]{0,2,1:T(8,128)(2,1)S(1)} %bitcast.81, bf16[512,2,16,64]{0,3,2,1:T(8,128)(2,1)} %bitcast.78), kind=kOutput, calls=%fused_computation.14 | convolution fusion | flops 549445632 | bytes 18907648 | tf_op jit(solution)/shard_map/while/body/eval_jaxpr/qhd,khd->hqk/dot_general | solution.py:24
  176.6 0.0 copy-start.6
  176.6 3.7 %fusion.15 = bf16[16,64,512]{2,1,0:T(8,128)(2,1)S(1)} fusion(f32[16,512,512]{1,2,0:T(8,128)S(1)} %get-tuple-element.84, f32[16,512]{1,0:T(8,128)S(1)} %get-tuple-element.83, pred[512]{0:T(512)(128)(4,1)S(1)} %iota_compare_fusion, bf16[512,2,16,64]{0,3,2,1:T(8,128)(2,1)S(1)} %bitcast.79), kind=kOutput, calls=%fused_computation.27 | convolution fusion | flops 554172416 | bytes 18907648 | tf_op jit(solution)/shard_map/while/body/eval_jaxpr/hqk,khd->qhd/dot_general | solution.py:29
  180.4 2.2 %fusion.16 = bf16[1,512,1024]{2,1,0:T(8,128)(2,1)} fusion(f32[512,1024]{1,0:T(8,128)S(1)} %copy-done.2, bf16[512,1024]{0,1:T(8,128)(2,1)S(1)} %bitcast.82, bf16[1024,1024]{1,0:T(8,128)(2,1)S(1)} %copy-done.6), kind=kOutput, calls=%fused_computation.29 | convolution fusion | flops 1074790400 | bytes 6291456 | tf_op jit(solution)/shard_map/dot_general | solution.py:76
  (21 shorter events, 0.0 us)
Async XLA Ops:
  6.5 152.7 %copy-start = (bf16[1024,1024]{1,0:T(8,128)(2,1)S(1)}, bf16[1024,1024]{1,0:T(8,128)(2,1)}, u32[]{:S(2)}) copy-start(bf16[1024,1024]{1,0:T(8,128)(2,1)} %param.19) | copy-start | bytes 6291460
  6.5 97.4 %all-gather.3.cloned.1.call-start = ((), (), s32[]{:S(2)}) async-start(), calls=%async_computation.2 | async-start | bytes 2359296 | tf_op jit(solution)/shard_map/all_gather | solution.py:68
  28.3 5.2 %copy-start.8 = (s32[8]{0:T(128)S(1)}, s32[8]{0:T(128)}, u32[]{:S(2)}) copy-start(s32[8]{0:T(128)} %param.16) | copy-start | bytes 100
  28.3 53.9 %all-to-all-start = ((bf16[512,3,1024]{0,1,2:T(4,128)(2,1)}), bf16[512,3,1024]{0,1,2:T(4,128)(2,1)}, u32[]{:S(2)}, u32[]{:S(2)}) async-start(bf16[512,3,1024]{0,1,2:T(4,128)(2,1)} %copy.29), calls=%async_computation | async-start | bytes 8388608 | tf_op jit(solution)/shard_map/all_to_all | solution.py:55
  33.3 133.8 %all-gather.5.cloned.1.call-start = ((), (), s32[]{:S(2)}) async-start(), calls=%async_computation.3 | async-start | bytes 2621440 | tf_op jit(solution)/shard_map/all_gather | solution.py:70
  107.8 38.9 %copy-start.9 = (s32[8]{0:T(128)S(1)}, s32[8]{0:T(128)}, u32[]{:S(2)}) copy-start(s32[8]{0:T(128)} %param.15) | copy-start | bytes 100
  107.8 4.1 %copy-start.4 = (bf16[2048,4,64]{0,2,1:T(8,128)(2,1)S(1)}, bf16[2048,4,64]{0,2,1:T(8,128)(2,1)}, u32[]{:S(2)}) copy-start(bf16[2048,4,64]{0,2,1:T(8,128)(2,1)} %get-tuple-element.136) | copy-start | bytes 3145732 | tf_op jit(solution)/shard_map/while
  116.2 4.1 %copy-start.4 = (bf16[2048,4,64]{0,2,1:T(8,128)(2,1)S(1)}, bf16[2048,4,64]{0,2,1:T(8,128)(2,1)}, u32[]{:S(2)}) copy-start(bf16[2048,4,64]{0,2,1:T(8,128)(2,1)} %get-tuple-element.136) | copy-start | bytes 3145732 | tf_op jit(solution)/shard_map/while
  124.6 4.0 %copy-start.4 = (bf16[2048,4,64]{0,2,1:T(8,128)(2,1)S(1)}, bf16[2048,4,64]{0,2,1:T(8,128)(2,1)}, u32[]{:S(2)}) copy-start(bf16[2048,4,64]{0,2,1:T(8,128)(2,1)} %get-tuple-element.136) | copy-start | bytes 3145732 | tf_op jit(solution)/shard_map/while
  132.9 4.0 %copy-start.4 = (bf16[2048,4,64]{0,2,1:T(8,128)(2,1)S(1)}, bf16[2048,4,64]{0,2,1:T(8,128)(2,1)}, u32[]{:S(2)}) copy-start(bf16[2048,4,64]{0,2,1:T(8,128)(2,1)} %get-tuple-element.136) | copy-start | bytes 3145732 | tf_op jit(solution)/shard_map/while
  141.3 18.0 %all-to-all-start.1 = ((bf16[4,512,256]{1,2,0:T(8,128)(2,1)}), bf16[4,512,256]{1,2,0:T(8,128)(2,1)S(1)}, u32[]{:S(2)}, u32[]{:S(2)}) async-start(bf16[4,512,256]{1,2,0:T(8,128)(2,1)} %bitcast.80), calls=%async_computation.1 | async-start | bytes 2097152 | tf_op jit(solution)/shard_map/all_to_all | solution.py:60
  159.2 4.1 %copy-start.5 = (bf16[1024,1024]{1,0:T(8,128)(2,1)S(1)}, bf16[1024,1024]{1,0:T(8,128)(2,1)}, u32[]{:S(2)}) copy-start(bf16[1024,1024]{1,0:T(8,128)(2,1)} %param.21) | copy-start | bytes 6291460
  159.2 4.1 %copy-start.7 = (f32[1024]{0:T(1024)S(1)}, f32[1024]{0:T(1024)}, u32[]{:S(2)}) copy-start(f32[1024]{0:T(1024)} %param.20) | copy-start | bytes 12292
  162.0 1.3 copy-start.1
  171.0 5.5 %copy-start.3 = (bf16[512,2048]{0,1:T(8,128)(2,1)S(1)}, bf16[512,2048]{0,1:T(8,128)(2,1)}, u32[]{:S(2)}) copy-start(bf16[512,2048]{0,1:T(8,128)(2,1)} %copy.33) | copy-start | bytes 6291460
  176.6 3.8 %copy-start.2 = (f32[512,1024]{1,0:T(8,128)S(1)}, f32[512,1024]{1,0:T(8,128)}, u32[]{:S(2)}) copy-start(f32[512,1024]{1,0:T(8,128)} %copy-done.1) | copy-start | bytes 6291460
  176.6 3.8 %copy-start.6 = (bf16[1024,1024]{1,0:T(8,128)(2,1)S(1)}, bf16[1024,1024]{1,0:T(8,128)(2,1)}, u32[]{:S(2)}) copy-start(bf16[1024,1024]{1,0:T(8,128)(2,1)} %param.23) | copy-start | bytes 6291460
Sparse Core Ops, SparseCore 0:
  9.5 51.9 all-gather.2
  107.9 23.6 all-gather.4
where the time goes:
time: 190 us; the launch traced here: 189 us
  matrix products  62 us (33%)
  waiting for transfers between devices  58.4 us (31%)
  local copies, waits for them, and re-layouts  41 us (22%)
  between operations  16.9 us (9%)
  starting transfers between devices  8.93 us (5%)
  other arithmetic  2.16 us (1%)
    all_to_all x1, waiting for transfers between devices, per_device(): lax.all_to_all(stacked, 'seq', split_axis=2, concat_axis=0, tiled=True)  46.4 us
    dot_general x5, matrix products, one_block(): jnp.einsum('qhd,khd->hqk', query_block, keys, preferred_element_type=jnp....  21.7 us
    dot_general x5, matrix products, one_block(): jnp.einsum('hqk,khd->qhd', weights, values, preferred_element_type=jnp.fl...  20.9 us
    all_to_all x1, waiting for transfers between devices, per_device(): lax.all_to_all(attended, 'seq', split_axis=0, concat_axis=1, tiled=True)  11.3 us
    dot_general x1, matrix products, per_device(): jnp.dot(normed, w_qkv, preferred_element_type=jnp.float32)  8.28 us
    all_to_all x2, local copies, waits for them, and re-layouts, per_device(): lax.all_to_all(stacked, 'seq', split_axis=2, concat_axis=0, tiled=True)  7.07 us
    reshape x1, local copies, waits for them, and re-layouts, per_device(): stacked = projected.reshape(tok_rows, 3, D)  6.53 us
    reshape x1, local copies, waits for them, and re-layouts, per_device(): split = local_heads.reshape(seq_rows, 3, head_count, HEAD_DIM)  6.1 us
  transfers between devices with their start and end apart: 4, of which 2 were waited for; matrix products, arithmetic and copies ran while one was open for 45% of the time, Pallas kernels for 0%

commit v1 on v0

--- a/solution.py
+++ b/solution.py
@@ -52,7 +52,16 @@
     normed = normalize(tokens, norm_gain).astype(jnp.bfloat16)
     projected = jnp.dot(normed, w_qkv, preferred_element_type=jnp.float32).astype(jnp.bfloat16)
     stacked = projected.reshape(tok_rows, 3, D)
-    local_heads = lax.all_to_all(stacked, "seq", split_axis=2, concat_axis=0, tiled=True)
+
+    def draw_slices_by_axis(t0, lane_axis):
+        z1 = jax.lax.psum(1, lane_axis)
+        vec_out = jnp.split(t0, z1, 2)
+        block_next = jnp.stack(vec_out, 0)
+        seen_now = jax.lax.all_to_all(block_next, lane_axis, 0, 0)
+        finding = jnp.concatenate(seen_now, 0)
+        return finding
+
+    local_heads = draw_slices_by_axis(stacked, "seq")
     seq_rows = local_heads.shape[0]
     split = local_heads.reshape(seq_rows, 3, head_count, HEAD_DIM)
     every = jnp.ones((seq_rows,), dtype=bool)

time: 190 us -> 175 us (0.921)
  waiting for transfers between devices: 58.4 us -> 47.4 us
  local copies, waits for them, and re-layouts: 41 us -> 35.5 us
    reshape x2 -> x0, local copies, waits for them, and re-layouts: 12.6 us -> none  [the longest x1 6.53 us: per_device(): stacked = projected.reshape(tok_rows, 3, D)]
    all_to_all x1, waiting for transfers between devices: 46.4 us -> 35.3 us  [draw_slices_by_axis(): seen_now = jax.lax.all_to_all(block_next, lane_axis, 0, 0)]
    another operation x0 -> x2, local copies, waits for them, and re-layouts: none -> 8.15 us  [the longest x1 6.1 us: per_device(): split = local_heads.reshape(seq_rows, 3, head_count, HEAD_DIM)]
    another operation x0 -> x1, other arithmetic: none -> 1.9 us  [draw_slices_by_axis(): block_next = jnp.stack(vec_out, 0)]
    all_to_all x2 -> x1, local copies, waits for them, and re-layouts: 7.07 us -> 5.98 us  [draw_slices_by_axis(): seen_now = jax.lax.all_to_all(block_next, lane_axis, 0, 0)]
  transfers between devices with their start and end apart: 4 -> 4, of which waited for: 2 -> 2; matrix products, arithmetic and copies ran while one was open for 45% -> 46% of each run, Pallas kernels for 0% -> 0%
where the time goes in v1:
time: 175 us; the launch traced here: 174 us
  matrix products  62 us (35%)
  waiting for transfers between devices  47.4 us (27%)
  local copies, waits for them, and re-layouts  35.5 us (20%)
  between operations  16.9 us (10%)
  starting transfers between devices  8.54 us (5%)
  other arithmetic  4.03 us (2%)
    all_to_all x1, waiting for transfers between devices, draw_slices_by_axis(): seen_now = jax.lax.all_to_all(block_next, lane_axis, 0, 0)  35.3 us
    dot_general x5, matrix products, one_block(): jnp.einsum('qhd,khd->hqk', query_block, keys, preferred_element_type=jnp....  21.7 us
    dot_general x5, matrix products, one_block(): jnp.einsum('hqk,khd->qhd', weights, values, preferred_element_type=jnp.fl...  20.9 us
    all_to_all x1, waiting for transfers between devices, per_device(): lax.all_to_all(attended, 'seq', split_axis=0, concat_axis=1, tiled=True)  11.3 us
    dot_general x1, matrix products, per_device(): jnp.dot(normed, w_qkv, preferred_element_type=jnp.float32)  8.28 us
    another operation x1, local copies, waits for them, and re-layouts, per_device(): split = local_heads.reshape(seq_rows, 3, head_count, HEAD_DIM)  6.1 us
    all_to_all x1, local copies, waits for them, and re-layouts, draw_slices_by_axis(): seen_now = jax.lax.all_to_all(block_next, lane_axis, 0, 0)  5.98 us
    all_to_all x1, starting transfers between devices, draw_slices_by_axis(): seen_now = jax.lax.all_to_all(block_next, lane_axis, 0, 0)  4.8 us
  transfers between devices with their start and end apart: 4, of which 2 were waited for; matrix products, arithmetic and copies ran while one was open for 46% of the time, Pallas kernels for 0%

profile of v1, /device:TPU:0, one launch (start us, length us, event | category | flops | bytes accessed | tf_op | source)
XLA Modules:
  0.0 174.4 jit_solution(8106904559421201490)
XLA Ops:
  6.5 0.0 all-gather.3.cloned.1.call-start
  6.5 0.7 all-gather.3.cloned.1.call-update
  7.3 1.5 fusion.12
  8.8 8.3 %convolution_convert_fusion = bf16[512,3072]{1,0:T(8,128)(2,1)} fusion(bf16[1024,3072]{1,0:T(8,128)(2,1)} %param.18, bf16[1,512,1024]{2,1,0:T(8,128)(2,1)} %param.13, f32[1024]{0:T(1024)} %param.17, f32[512]{0:T(512)S(1)} %add_rsqrt_fusion.1), kind=kOutput, calls=%fused_computation.16 | convolution fusion | flops 3224895488 | bytes 10491904 | tf_op jit(solution)/shard_map/dot_general | solution.py:53
  17.1 4.7 %copy.28 = bf16[512,3072]{0,1:T(8,128)(2,1)} copy(bf16[512,3072]{1,0:T(8,128)(2,1)} %convolution_convert_fusion) | data formatting | bytes 6291456 | tf_op jit(solution)/shard_map/convert_element_type | solution.py:53
  21.8 2.0 %slice_bitcast_fusion.9 = (bf16[1,512,3,256]{1,3,2,0:T(8,128)(2,1)S(1)}, bf16[1,512,3,256]{1,3,2,0:T(8,128)(2,1)S(1)}, bf16[1,512,3,256]{1,3,2,0:T(8,128)(2,1)S(1)}, bf16[1,512,3,256]{1,3,2,0:T(8,128)(2,1)S(1)}) fusion(bf16[512,3,1024]{0,2,1:T(8,128)(2,1)} %bitcast.80), kind=kLoop, calls=%fused_computation.44 | loop fusion | bytes 6291456 | tf_op jit(solution)/shard_map/stack | solution.py:59
  23.8 1.9 %pad_maximum_fusion = bf16[4,512,3,256]{1,3,2,0:T(8,128)(2,1)} fusion(bf16[1,512,3,256]{1,3,2,0:T(8,128)(2,1)S(1)} %get-tuple-element.82, bf16[1,512,3,256]{1,3,2,0:T(8,128)(2,1)S(1)} %get-tuple-element.83, bf16[1,512,3,256]{1,3,2,0:T(8,128)(2,1)S(1)} %get-tuple-element.84, bf16[1,512,3,256]{1,3,2,0:T(8,128)(2,1)S(1)} %get-tuple-element.81), kind=kLoop, calls=%fused_computation.17 | loop fusion | flops 4718592 | bytes 6291456 | tf_op jit(solution)/shard_map/stack | solution.py:59
  25.7 4.8 %all-to-all-start = ((bf16[4,512,3,256]{1,3,2,0:T(8,128)(2,1)}), bf16[4,512,3,256]{1,3,2,0:T(8,128)(2,1)}, u32[]{:S(2)}, u32[]{:S(2)}) async-start(bf16[4,512,3,256]{1,3,2,0:T(8,128)(2,1)} %pad_maximum_fusion), calls=%async_computation | async-start | bytes 6291456 | tf_op jit(solution)/shard_map/all_to_all | solution.py:60
  30.5 0.0 all-gather.5.cloned.1.call-start
  30.6 0.6 dynamic_slice.18
  32.9 35.3 %all-to-all-done = bf16[4,512,3,256]{1,3,2,0:T(8,128)(2,1)} async-done(((bf16[4,512,3,256]{1,3,2,0:T(8,128)(2,1)}), bf16[4,512,3,256]{1,3,2,0:T(8,128)(2,1)}, u32[]{:S(2)}, u32[]{:S(2)}) %all-to-all-start) | async-done | bytes 3145760 | tf_op jit(solution)/shard_map/all_to_all | solution.py:60
  68.1 6.0 %copy.29 = bf16[4,512,3,256]{1,0,3,2:T(4,128)(2,1)} copy(bf16[4,512,3,256]{1,3,2,0:T(8,128)(2,1)} %all-to-all-done) | data formatting | bytes 6291456 | tf_op jit(solution)/shard_map/all_to_all | solution.py:60
  74.1 6.1 %reshape_reshape.4 = bf16[2048,3,4,64]{0,3,2,1:T(8,128)(2,1)} reshape(bf16[4,512,3,256]{1,0,3,2:T(4,128)(2,1)} %copy.29) | data formatting | bytes 6291456 | tf_op jit(solution)/shard_map/reshape;reshape | solution.py:66
  80.2 3.6 %slice_bitcast_fusion.4 = (bf16[2048,4,64]{0,2,1:T(8,128)(2,1)}, bf16[2048,4,64]{0,2,1:T(8,128)(2,1)S(1)}, bf16[2048,1,4,64]{0,3,2,1:T(8,128)(2,1)}) fusion(bf16[2048,3,4,64]{0,3,2,1:T(8,128)(2,1)} %reshape_reshape.4), kind=kLoop, calls=%fused_computation.34 | loop fusion | bytes 6291456 | tf_op jit(solution)/shard_map/squeeze | solution.py:68
  83.8 2.6 %reshape_squeeze.3 = bf16[4,512,4,64]{1,0,3,2:T(4,128)(2,1)} reshape(bf16[2048,1,4,64]{0,3,2,1:T(8,128)(2,1)} %get-tuple-element.80) | data formatting | bytes 2097152 | tf_op jit(solution)/shard_map/reshape;squeeze | solution.py:33
  86.4 2.4 %copy.30 = bf16[4,512,4,64]{1,3,2,0:T(8,128)(2,1)} copy(bf16[4,512,4,64]{1,0,3,2:T(4,128)(2,1)} %reshape_squeeze.3) | data formatting | bytes 2097152 | tf_op jit(solution)/shard_map/while | solution.py:33
  88.9 3.8 %convolution_convert_fusion.1 = bf16[128,2048]{1,0:T(8,128)(2,1)} fusion(bf16[1024,2048]{1,0:T(8,128)(2,1)} %param.22, bf16[8,128,1024]{2,1,0:T(8,128)(2,1)} %all-gather.3.cloned.1.call-done, s32[]{:T(128)S(6)} %min.4, pred[]{:T(512)S(6)} %and.4), kind=kOutput, calls=%fused_computation.21 | convolution fusion | flops 537264128 | bytes 4980741 | tf_op jit(solution)/shard_map/dot_general | solution.py:78
  92.7 0.0 all-gather.5.cloned.1.call-update
  92.7 0.0 copy-start.9
  92.7 33.5 %while.2 = (s32[]{:T(128)}, bf16[4,512,4,64]{1,3,2,0:T(8,128)(2,1)}, bf16[4,512,4,64]{1,3,2,0:T(8,128)(2,1)}, bf16[2048,4,64]{0,2,1:T(8,128)(2,1)S(1)}, bf16[2048,4,64]{0,2,1:T(8,128)(2,1)}, /*index=5*/s32[]{:T(128)}) while((s32[]{:T(128)}, bf16[4,512,4,64]{1,3,2,0:T(8,128)(2,1)}, bf16[4,512,4,64]{1,3,2,0:T(8,128)(2,1)}, ...), condition=%wide.region_3.4_spmd, body=%wide.region_1.3_spmd.sunk | while | flops 1094842368 | bytes 40387680 | solution.py:33
  92.7 4.0 %fusion.49 = (f32[4,512]{1,0:T(4,128)S(1)}, f32[4,512,2048]{2,1,0:T(8,128)S(1)}) fusion(bf16[2048,4,64]{0,2,1:T(8,128)(2,1)S(1)} %get-tuple-element.139, bf16[4,512,4,64]{1,3,2,0:T(8,128)(2,1)} %get-tuple-element.138, s32[]{:T(128)} %get-tuple-element.130), kind=kOutput, calls=%fused_computation.2.clone.1 | convolution fusion | flops 545257472 | bytes 18096640 | tf_op jit(solution)/shard_map/while/body/eval_jaxpr/qhd,khd->hqk/dot_general | solution.py:24
  96.8 0.0 copy-done.4
  96.8 4.3 %fusion.50 = bf16[4,512,4,64]{1,3,2,0:T(8,128)(2,1)} fusion(bf16[4,512,4,64]{1,3,2,0:T(8,128)(2,1)} %get-tuple-element.131, s32[]{:T(128)} %get-tuple-element.130, bf16[2048,4,64]{0,2,1:T(8,128)(2,1)S(1)} %copy-done.4, f32[4,512,2048]{2,1,0:T(8,128)S(1)} %get-tuple-element.122, f32[4,512]{1,0:T(4,128)S(1)} %get-tuple-element.123), kind=kOutput, calls=%fused_computation.6.clone.1 | convolution fusion | flops 549584896 | bytes 18096640 | tf_op jit(solution)/shard_map/while/body/eval_jaxpr/hqk,khd->qhd/dot_general | solution.py:29
  101.1 4.1 %fusion.49 = (f32[4,512]{1,0:T(4,128)S(1)}, f32[4,512,2048]{2,1,0:T(8,128)S(1)}) fusion(bf16[2048,4,64]{0,2,1:T(8,128)(2,1)S(1)} %get-tuple-element.139, bf16[4,512,4,64]{1,3,2,0:T(8,128)(2,1)} %get-tuple-element.138, s32[]{:T(128)} %get-tuple-element.130), kind=kOutput, calls=%fused_computation.2.clone.1 | convolution fusion | flops 545257472 | bytes 18096640 | tf_op jit(solution)/shard_map/while/body/eval_jaxpr/qhd,khd->hqk/dot_general | solution.py:24
  105.1 0.0 copy-done.4
  105.2 4.3 %fusion.50 = bf16[4,512,4,64]{1,3,2,0:T(8,128)(2,1)} fusion(bf16[4,512,4,64]{1,3,2,0:T(8,128)(2,1)} %get-tuple-element.131, s32[]{:T(128)} %get-tuple-element.130, bf16[2048,4,64]{0,2,1:T(8,128)(2,1)S(1)} %copy-done.4, f32[4,512,2048]{2,1,0:T(8,128)S(1)} %get-tuple-element.122, f32[4,512]{1,0:T(4,128)S(1)} %get-tuple-element.123), kind=kOutput, calls=%fused_computation.6.clone.1 | convolution fusion | flops 549584896 | bytes 18096640 | tf_op jit(solution)/shard_map/while/body/eval_jaxpr/hqk,khd->qhd/dot_general | solution.py:29
  109.5 4.0 %fusion.49 = (f32[4,512]{1,0:T(4,128)S(1)}, f32[4,512,2048]{2,1,0:T(8,128)S(1)}) fusion(bf16[2048,4,64]{0,2,1:T(8,128)(2,1)S(1)} %get-tuple-element.139, bf16[4,512,4,64]{1,3,2,0:T(8,128)(2,1)} %get-tuple-element.138, s32[]{:T(128)} %get-tuple-element.130), kind=kOutput, calls=%fused_computation.2.clone.1 | convolution fusion | flops 545257472 | bytes 18096640 | tf_op jit(solution)/shard_map/while/body/eval_jaxpr/qhd,khd->hqk/dot_general | solution.py:24
  113.5 4.3 %fusion.50 = bf16[4,512,4,64]{1,3,2,0:T(8,128)(2,1)} fusion(bf16[4,512,4,64]{1,3,2,0:T(8,128)(2,1)} %get-tuple-element.131, s32[]{:T(128)} %get-tuple-element.130, bf16[2048,4,64]{0,2,1:T(8,128)(2,1)S(1)} %copy-done.4, f32[4,512,2048]{2,1,0:T(8,128)S(1)} %get-tuple-element.122, f32[4,512]{1,0:T(4,128)S(1)} %get-tuple-element.123), kind=kOutput, calls=%fused_computation.6.clone.1 | convolution fusion | flops 549584896 | bytes 18096640 | tf_op jit(solution)/shard_map/while/body/eval_jaxpr/hqk,khd->qhd/dot_general | solution.py:29
  117.8 4.0 %fusion.49 = (f32[4,512]{1,0:T(4,128)S(1)}, f32[4,512,2048]{2,1,0:T(8,128)S(1)}) fusion(bf16[2048,4,64]{0,2,1:T(8,128)(2,1)S(1)} %get-tuple-element.139, bf16[4,512,4,64]{1,3,2,0:T(8,128)(2,1)} %get-tuple-element.138, s32[]{:T(128)} %get-tuple-element.130), kind=kOutput, calls=%fused_computation.2.clone.1 | convolution fusion | flops 545257472 | bytes 18096640 | tf_op jit(solution)/shard_map/while/body/eval_jaxpr/qhd,khd->hqk/dot_general | solution.py:24
  121.9 4.3 %fusion.50 = bf16[4,512,4,64]{1,3,2,0:T(8,128)(2,1)} fusion(bf16[4,512,4,64]{1,3,2,0:T(8,128)(2,1)} %get-tuple-element.131, s32[]{:T(128)} %get-tuple-element.130, bf16[2048,4,64]{0,2,1:T(8,128)(2,1)S(1)} %copy-done.4, f32[4,512,2048]{2,1,0:T(8,128)S(1)} %get-tuple-element.122, f32[4,512]{1,0:T(4,128)S(1)} %get-tuple-element.123), kind=kOutput, calls=%fused_computation.6.clone.1 | convolution fusion | flops 549584896 | bytes 18096640 | tf_op jit(solution)/shard_map/while/body/eval_jaxpr/hqk,khd->qhd/dot_general | solution.py:29
  126.2 3.7 %all-to-all-start.1 = ((bf16[4,512,256]{1,2,0:T(8,128)(2,1)}), bf16[4,512,256]{1,2,0:T(8,128)(2,1)S(1)}, u32[]{:S(2)}, u32[]{:S(2)}) async-start(bf16[4,512,256]{1,2,0:T(8,128)(2,1)} %bitcast.12), calls=%async_computation.1 | async-start | bytes 2097152 | tf_op jit(solution)/shard_map/all_to_all | solution.py:69
  131.5 0.0 copy-done.9
  131.5 0.6 dynamic_slice.20
  132.2 0.6 iota_compare_fusion
  132.8 11.3 %all-to-all-done.1 = bf16[4,512,256]{1,2,0:T(8,128)(2,1)S(1)} async-done(((bf16[4,512,256]{1,2,0:T(8,128)(2,1)}), bf16[4,512,256]{1,2,0:T(8,128)(2,1)S(1)}, u32[]{:S(2)}, u32[]{:S(2)}) %all-to-all-start.1) | async-done | bytes 1048608 | tf_op jit(solution)/shard_map/all_to_all | solution.py:69
  144.1 2.7 %multiply_reduce_fusion = (f32[512]{0:T(512)S(1)}, f32[512,1024]{1,0:T(8,128)S(1)}) fusion(bf16[512,1024]{0,1:T(8,128)(2,1)S(1)} %bitcast.81, bf16[1024,1024]{1,0:T(8,128)(2,1)S(1)} %copy-done, bf16[1,512,1024]{2,1,0:T(8,128)(2,1)} %param.13), kind=kOutput, calls=%fused_computation.27 | convolution fusion | flops 1075838464 | bytes 6293504 | tf_op jit(solution)/shard_map/dot_general | solution.py:70
  146.9 1.3 copy-done.1
  148.2 0.0 copy-done.5
  148.2 2.3 %convolution_convert_fusion.2 = bf16[512,1024]{1,0:T(8,128)(2,1)} fusion(bf16[1024,1024]{1,0:T(8,128)(2,1)S(1)} %copy-done.5, f32[512,1024]{1,0:T(8,128)S(1)} %get-tuple-element.86, f32[1024]{0:T(1024)S(1)} %copy-done.7, f32[512]{0:T(512)S(1)} %add_rsqrt_fusion), kind=kOutput, calls=%fused_computation.29 | convolution fusion | flops 1075838976 | bytes 5249024 | tf_op jit(solution)/shard_map/dot_general | solution.py:72
  150.5 1.5 copy.32
  152.0 0.0 all-gather.5.cloned.1.call-done
  152.0 3.9 %copy.31 = bf16[512,2048]{0,1:T(8,128)(2,1)} copy(bf16[512,2048]{1,0:T(8,128)(2,1)} %all-gather.5.cloned.1.call-done) | data formatting | bytes 4194304 | tf_op jit(solution)/shard_map/all_gather | solution.py:79
  156.0 5.5 %fusion.10 = (f32[16,512]{1,0:T(8,128)S(1)}, f32[16,512,512]{1,2,0:T(8,128)S(1)}) fusion(pred[512]{0:T(512)(128)(4,1)S(1)} %iota_compare_fusion, bf16[512,16,64]{0,2,1:T(8,128)(2,1)S(1)} %bitcast.84, bf16[512,2,16,64]{0,3,2,1:T(8,128)(2,1)} %bitcast.82), kind=kOutput, calls=%fused_computation.14 | convolution fusion | flops 549445632 | bytes 18907648 | tf_op jit(solution)/shard_map/while/body/eval_jaxpr/qhd,khd->hqk/dot_general | solution.py:24
  161.5 0.0 copy-start.6
  161.5 3.7 %fusion.15 = bf16[16,64,512]{2,1,0:T(8,128)(2,1)S(1)} fusion(f32[16,512,512]{1,2,0:T(8,128)S(1)} %get-tuple-element.88, f32[16,512]{1,0:T(8,128)S(1)} %get-tuple-element.87, pred[512]{0:T(512)(128)(4,1)S(1)} %iota_compare_fusion, bf16[512,2,16,64]{0,3,2,1:T(8,128)(2,1)S(1)} %bitcast.83), kind=kOutput, calls=%fused_computation.28 | convolution fusion | flops 554172416 | bytes 18907648 | tf_op jit(solution)/shard_map/while/body/eval_jaxpr/hqk,khd->qhd/dot_general | solution.py:29
  165.3 0.0 copy-done.2
  165.3 0.0 copy-done.6
  165.3 2.2 %fusion.16 = bf16[1,512,1024]{2,1,0:T(8,128)(2,1)} fusion(f32[512,1024]{1,0:T(8,128)S(1)} %copy-done.2, bf16[512,1024]{0,1:T(8,128)(2,1)S(1)} %bitcast.85, bf16[1024,1024]{1,0:T(8,128)(2,1)S(1)} %copy-done.6), kind=kOutput, calls=%fused_computation.30 | convolution fusion | flops 1074790400 | bytes 6291456 | tf_op jit(solution)/shard_map/dot_general | solution.py:85
  (21 shorter events, 0.0 us)
Async XLA Ops:
  6.5 137.6 %copy-start = (bf16[1024,1024]{1,0:T(8,128)(2,1)S(1)}, bf16[1024,1024]{1,0:T(8,128)(2,1)}, u32[]{:S(2)}) copy-start(bf16[1024,1024]{1,0:T(8,128)(2,1)} %param.19) | copy-start | bytes 6291460
  6.5 82.3 %all-gather.3.cloned.1.call-start = ((), (), s32[]{:S(2)}) async-start(), calls=%async_computation.2 | async-start | bytes 2359296 | tf_op jit(solution)/shard_map/all_gather | solution.py:77
  25.7 4.9 %copy-start.8 = (s32[8]{0:T(128)S(1)}, s32[8]{0:T(128)}, u32[]{:S(2)}) copy-start(s32[8]{0:T(128)} %param.16) | copy-start | bytes 100
  25.7 42.4 %all-to-all-start = ((bf16[4,512,3,256]{1,3,2,0:T(8,128)(2,1)}), bf16[4,512,3,256]{1,3,2,0:T(8,128)(2,1)}, u32[]{:S(2)}, u32[]{:S(2)}) async-start(bf16[4,512,3,256]{1,3,2,0:T(8,128)(2,1)} %pad_maximum_fusion), calls=%async_computation | async-start | bytes 6291456 | tf_op jit(solution)/shard_map/all_to_all | solution.py:60
  30.5 121.5 %all-gather.5.cloned.1.call-start = ((), (), s32[]{:S(2)}) async-start(), calls=%async_computation.3 | async-start | bytes 2621440 | tf_op jit(solution)/shard_map/all_gather | solution.py:79
  92.7 38.9 %copy-start.9 = (s32[8]{0:T(128)S(1)}, s32[8]{0:T(128)}, u32[]{:S(2)}) copy-start(s32[8]{0:T(128)} %param.15) | copy-start | bytes 100
  92.7 4.1 %copy-start.4 = (bf16[2048,4,64]{0,2,1:T(8,128)(2,1)S(1)}, bf16[2048,4,64]{0,2,1:T(8,128)(2,1)}, u32[]{:S(2)}) copy-start(bf16[2048,4,64]{0,2,1:T(8,128)(2,1)} %get-tuple-element.140) | copy-start | bytes 3145732 | tf_op jit(solution)/shard_map/while
  101.1 4.1 %copy-start.4 = (bf16[2048,4,64]{0,2,1:T(8,128)(2,1)S(1)}, bf16[2048,4,64]{0,2,1:T(8,128)(2,1)}, u32[]{:S(2)}) copy-start(bf16[2048,4,64]{0,2,1:T(8,128)(2,1)} %get-tuple-element.140) | copy-start | bytes 3145732 | tf_op jit(solution)/shard_map/while
  109.5 4.0 %copy-start.4 = (bf16[2048,4,64]{0,2,1:T(8,128)(2,1)S(1)}, bf16[2048,4,64]{0,2,1:T(8,128)(2,1)}, u32[]{:S(2)}) copy-start(bf16[2048,4,64]{0,2,1:T(8,128)(2,1)} %get-tuple-element.140) | copy-start | bytes 3145732 | tf_op jit(solution)/shard_map/while
  117.8 4.0 %copy-start.4 = (bf16[2048,4,64]{0,2,1:T(8,128)(2,1)S(1)}, bf16[2048,4,64]{0,2,1:T(8,128)(2,1)}, u32[]{:S(2)}) copy-start(bf16[2048,4,64]{0,2,1:T(8,128)(2,1)} %get-tuple-element.140) | copy-start | bytes 3145732 | tf_op jit(solution)/shard_map/while
  126.2 18.0 %all-to-all-start.1 = ((bf16[4,512,256]{1,2,0:T(8,128)(2,1)}), bf16[4,512,256]{1,2,0:T(8,128)(2,1)S(1)}, u32[]{:S(2)}, u32[]{:S(2)}) async-start(bf16[4,512,256]{1,2,0:T(8,128)(2,1)} %bitcast.12), calls=%async_computation.1 | async-start | bytes 2097152 | tf_op jit(solution)/shard_map/all_to_all | solution.py:69
  144.1 4.1 %copy-start.5 = (bf16[1024,1024]{1,0:T(8,128)(2,1)S(1)}, bf16[1024,1024]{1,0:T(8,128)(2,1)}, u32[]{:S(2)}) copy-start(bf16[1024,1024]{1,0:T(8,128)(2,1)} %param.21) | copy-start | bytes 6291460
  144.1 4.1 %copy-start.7 = (f32[1024]{0:T(1024)S(1)}, f32[1024]{0:T(1024)}, u32[]{:S(2)}) copy-start(f32[1024]{0:T(1024)} %param.20) | copy-start | bytes 12292
  146.9 1.3 copy-start.1
  156.0 5.5 %copy-start.3 = (bf16[512,2048]{0,1:T(8,128)(2,1)S(1)}, bf16[512,2048]{0,1:T(8,128)(2,1)}, u32[]{:S(2)}) copy-start(bf16[512,2048]{0,1:T(8,128)(2,1)} %copy.31) | copy-start | bytes 6291460
  161.5 3.8 %copy-start.2 = (f32[512,1024]{1,0:T(8,128)S(1)}, f32[512,1024]{1,0:T(8,128)}, u32[]{:S(2)}) copy-start(f32[512,1024]{1,0:T(8,128)} %copy-done.1) | copy-start | bytes 6291460
  161.5 3.8 %copy-start.6 = (bf16[1024,1024]{1,0:T(8,128)(2,1)S(1)}, bf16[1024,1024]{1,0:T(8,128)(2,1)}, u32[]{:S(2)}) copy-start(bf16[1024,1024]{1,0:T(8,128)(2,1)} %param.23) | copy-start | bytes 6291460
Sparse Core Ops, SparseCore 0:
  9.5 51.9 all-gather.2
  92.8 23.7 all-gather.4
